TPU v7x, 32 devices: a whole 2x2x4 slice. The times are simulated.
32 devices in a mesh: groups: 2 (over x), row: 16 (over z, y, core).
Axes of the slice: x: 2, y: 2, z: 4, core: 2. Of those that a mesh axis runs over, the one named last changes fastest.
Arguments:
- pair_rows: bfloat16 [256, 128, 128], P(('groups', 'row')), parts along dimension 0, may hold values from -6 to 6
- in_gain: float32 [128], replicated, may hold values from 0.1 to 1.9
- w_left: bfloat16 [128, 128], replicated, may hold values from -0.5 to 0.5
- w_left_gate: bfloat16 [128, 128], replicated, may hold values from -0.5 to 0.5
- w_right: bfloat16 [128, 128], replicated, may hold values from -0.5 to 0.5
- w_right_gate: bfloat16 [128, 128], replicated, may hold values from -0.5 to 0.5
- w_gate: bfloat16 [128, 128], replicated, may hold values from -0.5 to 0.5
- w_out: bfloat16 [128, 128], replicated, may hold values from -0.5 to 0.5
- out_gain: float32 [128], replicated, may hold values from 0.1 to 1.9
- valid_len: int32 [2], P('groups'), parts along dimension 0, may hold values from 64 to 128
- window: int32 [2], P('groups'), parts along dimension 0, may hold values from 0 to 7
Outputs:
- update: bfloat16 [256, 16, 128], P(('groups', 'row')), parts along dimension 0
There are 2 independent parts, one for each index of `groups`. A program takes and returns all parts, laid end to end along the dimension named above; an argument that names none is the same for every part. Nothing has to cross between parts.
All inputs are finite; a program needn't handle non-finite values.
Results may differ from a plain program's by a relative error of at most 0.0078.
Values may be sent and summed in bfloat16 or wider, within the bound.
A program may use at most 128 MiB of HBM per device.

v0:
```python
import jax
import jax.numpy as jnp
from jax import lax
from jax.sharding import PartitionSpec as P


def layer_norm(values, gain):
    mean_v = jnp.mean(values, axis=-1, keepdims=True)
    centered = values - mean_v
    variance_v = jnp.mean(centered * centered, axis=-1, keepdims=True)
    return centered * lax.rsqrt(variance_v + 1e-05) * gain


def on_device(
    pair_rows,
    in_gain,
    w_left,
    w_left_gate,
    w_right,
    w_right_gate,
    w_gate,
    w_out,
    out_gain,
    valid_len,
    window,
):
    my_index = lax.axis_index("row")
    local_rows, tokens_all, channels = pair_rows.shape
    width_win = tokens_all // 8
    valid_upto = valid_len[0]
    start_block = window[0]
    start_row = start_block * width_win
    row_ids = my_index * local_rows + jnp.arange(local_rows, dtype=jnp.int32)
    row_live = (row_ids < valid_upto).astype(jnp.float32)
    col_live = (jnp.arange(tokens_all, dtype=jnp.int32) < valid_upto).astype(jnp.float32)
    live_mask = (row_live[:, None] * col_live[None, :])[:, :, None]
    normed = layer_norm(pair_rows.astype(jnp.float32), in_gain).astype(jnp.bfloat16)
    flat_rows = normed.reshape(-1, channels)
    joined = jnp.concatenate([w_left, w_left_gate, w_right, w_right_gate], axis=1)
    projected = jnp.dot(flat_rows, joined, preferred_element_type=jnp.float32)
    projected = projected.reshape(local_rows, tokens_all, 4 * channels)
    left_edge = (
        jax.nn.sigmoid(projected[:, :, channels : 2 * channels])
        * projected[:, :, :channels]
        * live_mask
    ).astype(jnp.bfloat16)
    right_edge = (
        jax.nn.sigmoid(projected[:, :, 3 * channels :])
        * projected[:, :, 2 * channels : 3 * channels]
        * live_mask
    ).astype(jnp.bfloat16)
    gate_in = lax.dynamic_slice_in_dim(normed, start_row, width_win, 1)
    gate_vals = jax.nn.sigmoid(
        jnp.dot(gate_in.reshape(-1, channels), w_gate, preferred_element_type=jnp.float32)
    )
    gate_vals = gate_vals.reshape(local_rows, width_win, channels)
    regrouped = lax.all_to_all(right_edge, "row", split_axis=1, concat_axis=0, tiled=True)
    picked = lax.dynamic_slice_in_dim(regrouped, start_row, width_win, 0)
    window_right = lax.all_gather(picked, "row", axis=1, tiled=True)
    product = jnp.einsum(
        "ikc,jkc->ijc", left_edge, window_right, preferred_element_type=jnp.float32
    )
    normed_out = layer_norm(product, out_gain).astype(jnp.bfloat16)
    result = jnp.dot(normed_out.reshape(-1, channels), w_out, preferred_element_type=jnp.float32)
    return (gate_vals * result.reshape(local_rows, width_win, channels)).astype(jnp.bfloat16)


def solution(mesh):
    return jax.shard_map(
        on_device,
        mesh=mesh,
        in_specs=(
            P(("groups", "row"), None, None),
            P(),
            P(),
            P(),
            P(),
            P(),
            P(),
            P(),
            P(),
            P("groups"),
            P("groups"),
        ),
        out_specs=P(("groups", "row"), None, None),
        check_vma=False,
    )
```

profile of v0, /device:TPU:0, one launch (start us, length us, event | category | flops | bytes accessed | tf_op | source)
XLA Modules:
  0.0 75.4 jit_solution(6741622553419118071)
XLA Ops:
  0.0 0.0 copy-start
  0.7 1.1 %convert_reduce_fusion = f32[8,128]{1,0:T(8,128)S(1)} fusion(bf16[8,128,128]{2,1,0:T(8,128)(2,1)} %param.11), kind=kLoop, calls=%fused_computation.7 | loop fusion | flops 261120 | bytes 266240 | tf_op jit(solution)/shard_map/reduce_sum | solution.py:8
  1.8 1.3 %fusion.6 = f32[8,128]{1,0:T(8,128)S(1)} fusion(bf16[8,128,128]{2,1,0:T(8,128)(2,1)} %param.11, f32[8,128]{1,0:T(8,128)S(1)} %broadcast_multiply_fusion.2), kind=kLoop, calls=%fused_computation.10 | loop fusion | flops 523264 | bytes 270336 | tf_op jit(solution)/shard_map/reduce_sum | solution.py:10
  3.1 0.1 broadcast_multiply_fusion.1
  3.2 1.3 %fusion.8 = bf16[8,128,128]{2,1,0:T(8,128)(2,1)S(1)} fusion(bf16[8,128,128]{2,1,0:T(8,128)(2,1)} %param.11, f32[128]{0:T(128)} %param.12, f32[8,128]{1,0:T(8,128)S(1)} %add_rsqrt_fusion.1, f32[8,128]{1,0:T(8,128)S(1)} %broadcast_multiply_fusion.2), kind=kLoop, calls=%fused_computation.12 | loop fusion | flops 655360 | bytes 532992 | tf_op jit(solution)/shard_map/convert_element_type | solution.py:37
  4.5 1.2 %fusion.19 = f32[8,128,512]{2,1,0:T(8,128)S(1)} fusion(bf16[8,128,128]{2,1,0:T(8,128)(2,1)S(1)} %fusion.8, bf16[128,128]{1,0:T(8,128)(2,1)} %param.16, bf16[128,128]{1,0:T(8,128)(2,1)} %param.15, bf16[128,128]{1,0:T(8,128)(2,1)} %param.14, bf16[128,128]{1,0:T(8,128)(2,1)} %param.13), kind=kOutput, calls=%fused_computation.28 | convolution fusion | flops 134742016 | bytes 2490368 | tf_op jit(solution)/shard_map/dot_general | solution.py:40
  5.7 0.3 fusion.10
  6.0 0.9 %copy.29 = bf16[8,128,128]{2,0,1:T(8,128)(2,1)} copy(bf16[8,128,128]{2,1,0:T(8,128)(2,1)S(1)} %get-tuple-element.6) | data formatting | bytes 524288 | tf_op jit(solution)/shard_map/convert_element_type | solution.py:51
  6.9 7.4 %all-to-all-start = ((bf16[8,128,128]{2,0,1:T(8,128)(2,1)}), bf16[8,128,128]{2,0,1:T(8,128)(2,1)S(1)}, u32[]{:S(2)}, u32[]{:S(2)}) async-start(bf16[8,128,128]{2,0,1:T(8,128)(2,1)} %copy.29), calls=%async_computation | async-start | bytes 524288 | tf_op jit(solution)/shard_map/all_to_all | solution.py:57
  15.0 0.2 copy.33
  15.2 0.0 copy-done
  15.2 0.2 fusion.2
  15.4 9.0 %all-to-all-done = bf16[8,128,128]{2,0,1:T(8,128)(2,1)S(1)} async-done(((bf16[8,128,128]{2,0,1:T(8,128)(2,1)}), bf16[8,128,128]{2,0,1:T(8,128)(2,1)S(1)}, u32[]{:S(2)}, u32[]{:S(2)}) %all-to-all-start) | async-done | bytes 262176 | tf_op jit(solution)/shard_map/all_to_all | solution.py:57
  24.4 0.2 copy.36
  24.6 0.0 copy-start.1
  24.6 0.0 copy-start.2
  24.6 48.2 %all_gather.3 = bf16[16,128,128]{0,1,2:T(8,128)(2,1)S(1)} all-gather(bf16[16,8,128]{0,1,2:T(8,128)(2,1)S(1)} %copy.36), channel_id=1, replica_groups=mesh['groups'=2,'row'=16] {'row'}, dimensions={1}, use_global_device_ids=true | all-gather | bytes 557056 | tf_op jit(solution)/shard_map/all_gather | solution.py:59
  72.9 1.2 %fusion.31 = f32[128,16,8]{1,2,0:T(8,128)S(1)} fusion(bf16[16,128,128]{0,1,2:T(8,128)(2,1)S(1)} %all_gather.3, bf16[8,128,128]{1,0,2:T(8,128)(2,1)S(1)} %copy.33), kind=kOutput, calls=%fused_computation.53 | convolution fusion | flops 4194304 | bytes 851968 | tf_op jit(solution)/shard_map/ikc,jkc->ijc/dot_general | solution.py:60
  74.1 0.2 copy.34
  74.3 0.1 bitcast_reduce_fusion
  74.4 0.2 multiply_reduce_fusion
  74.6 0.0 copy-done.1
  74.6 0.0 copy-done.2
  74.6 0.8 %fusion.3 = bf16[8,16,128]{2,1,0:T(8,128)(2,1)} fusion(f32[8,16,128]{2,1,0:T(8,128)S(1)} %bitcast.31, f32[128,16,8]{0,1,2:T(8,128)S(1)} %copy.34, bf16[128,128]{1,0:T(8,128)(2,1)S(1)} %copy-done.1, f32[128]{0:T(128)S(1)} %copy-done.2, f32[8,16]{1,0:T(8,128)S(1)} %add_rsqrt_fusion, f32[8,16]{1,0:T(8,128)S(1)} %broadcast_multiply_fusion), kind=kOutput, calls=%fused_computation.5 | convolution fusion | flops 4292608 | bytes 198144 | tf_op jit(solution)/shard_map/dot_general | solution.py:64
  (9 shorter events, 0.1 us)
Async XLA Ops:
  0.0 15.2 %copy-start = (bf16[128,128]{1,0:T(8,128)(2,1)S(1)}, bf16[128,128]{1,0:T(8,128)(2,1)}, u32[]{:S(2)}) copy-start(bf16[128,128]{1,0:T(8,128)(2,1)} %param.17) | copy-start | bytes 98308
  6.9 17.4 %all-to-all-start = ((bf16[8,128,128]{2,0,1:T(8,128)(2,1)}), bf16[8,128,128]{2,0,1:T(8,128)(2,1)S(1)}, u32[]{:S(2)}, u32[]{:S(2)}) async-start(bf16[8,128,128]{2,0,1:T(8,128)(2,1)} %copy.29), calls=%async_computation | async-start | bytes 524288 | tf_op jit(solution)/shard_map/all_to_all | solution.py:57
  24.6 49.9 %copy-start.1 = (bf16[128,128]{1,0:T(8,128)(2,1)S(1)}, bf16[128,128]{1,0:T(8,128)(2,1)}, u32[]{:S(2)}) copy-start(bf16[128,128]{1,0:T(8,128)(2,1)} %param.18) | copy-start | bytes 98308
  24.6 49.9 %copy-start.2 = (f32[128]{0:T(128)S(1)}, f32[128]{0:T(128)}, u32[]{:S(2)}) copy-start(f32[128]{0:T(128)} %param.19) | copy-start | bytes 1540
where the time goes:
time: 76 us; the launch traced here: 75.4 us
  blocking collectives  48.2 us (63%)
  waiting for transfers between devices  8.97 us (12%)
  starting transfers between devices  7.41 us (10%)
  other arithmetic  4.38 us (6%)
  matrix products  3.4 us (4%)
  local copies, waits for them, and re-layouts  1.53 us (2%)
  between operations  1.5 us (2%)
    all_gather x1, blocking collectives, on_device(): window_right = lax.all_gather(picked, 'row', axis=1, tiled=True)  48.2 us
    all_to_all x1, waiting for transfers between devices, on_device(): lax.all_to_all(right_edge, 'row', split_axis=1, concat_axis=0, tiled=True)  8.97 us
    all_to_all x1, starting transfers between devices, on_device(): lax.all_to_all(right_edge, 'row', split_axis=1, concat_axis=0, tiled=True)  7.41 us
  transfers between devices with their start and end apart: 1, of which 1 were waited for; matrix products, arithmetic and copies ran while one was open for 0% of the time, Pallas kernels for 0%

commit v1 on v0

--- a/solution.py
+++ b/solution.py
@@ -1,6 +1,10 @@
+import functools
+
 import jax
 import jax.numpy as jnp
 from jax import lax
+from jax.experimental import pallas as pl
+from jax.experimental.pallas import tpu as pltpu
 from jax.sharding import PartitionSpec as P
 
 
@@ -65,9 +69,281 @@
     return (gate_vals * result.reshape(local_rows, width_win, channels)).astype(jnp.bfloat16)
 
 
+MESH = pl.DeviceIdType.MESH
+CHUNKS = 4
+LINE = 4
+Y1, NEAR, EXCH, FAR, Y2, C1, C2 = range(7)
+
+
+def fused_kernel(
+    valid_ref,
+    window_ref,
+    x_ref,
+    in_gain_ref,
+    w_left_ref,
+    w_left_gate_ref,
+    w_right_ref,
+    w_right_gate_ref,
+    w_gate_ref,
+    w_out_ref,
+    out_gain_ref,
+    o_ref,
+    normed_ref,
+    left_ref,
+    right_ref,
+    from_y,
+    here,
+    near,
+    best,
+    other,
+    win_ref,
+    prod_ref,
+    send_sem,
+    recv_sem,
+):
+    local_rows, tokens, channels = x_ref.shape
+    half = tokens // 2
+    width = o_ref.shape[1]
+    step = local_rows // CHUNKS
+
+    me = lax.axis_index("row")
+    core = lax.rem(me, 2)
+    chip = lax.div(me, 2)
+    y = lax.rem(chip, 2)
+    z = lax.div(chip, 2)
+    zrem = lax.rem(z, 2)
+    zhalf = lax.div(z, 2)
+
+    def at(z_, y_, core_):
+        return {"row": (z_ * 2 + y_) * 2 + core_}
+
+    y_peer = at(z, 1 - y, core)
+    core_peer = at(z, y, 1 - core)
+    pair_peer = at(zhalf * 2 + 1 - zrem, y, core)
+    inner_peer = at(LINE - 1 - z, y, core)
+    outer = jnp.logical_or(z == 0, z == LINE - 1)
+    inner = jnp.logical_not(outer)
+    mine = pl.ds(pl.multiple_of(y * half, half), half)
+    theirs = pl.ds(pl.multiple_of((1 - y) * half, half), half)
+
+    def copy(kind, q):
+        rows = pl.ds(q * step, step)
+        src, dst, dev = {
+            Y1: (right_ref.at[rows, theirs], from_y.at[rows], y_peer),
+            NEAR: (here.at[rows], near.at[rows], pair_peer),
+            EXCH: (best.at[rows], other.at[rows], inner_peer),
+            FAR: (win_ref.at[core, rows, mine], win_ref.at[core, rows, mine], pair_peer),
+            Y2: (win_ref.at[core, rows, mine], win_ref.at[core, rows, mine], y_peer),
+            C1: (win_ref.at[core, rows, mine], win_ref.at[core, rows, mine], core_peer),
+            C2: (win_ref.at[core, rows, theirs], win_ref.at[core, rows, theirs], core_peer),
+        }[kind]
+        return pltpu.make_async_remote_copy(
+            src_ref=src,
+            dst_ref=dst,
+            send_sem=send_sem.at[kind, q],
+            recv_sem=recv_sem.at[kind, q],
+            device_id=dev,
+            device_id_type=MESH,
+        )
+
+    barrier = pltpu.get_barrier_semaphore()
+    for peer in (y_peer, core_peer, pair_peer):
+        pl.semaphore_signal(barrier, inc=1, device_id=peer, device_id_type=MESH)
+
+    @pl.when(inner)
+    def _():
+        pl.semaphore_signal(barrier, inc=1, device_id=inner_peer, device_id_type=MESH)
+        pl.semaphore_wait(barrier, 4)
+
+    @pl.when(outer)
+    def _():
+        pl.semaphore_wait(barrier, 3)
+
+    win = window_ref[0]
+    win_v = jnp.full((half, channels), win, jnp.int32)
+
+    def flag(cond):
+        return jnp.where(cond, 1.0, 0.0).astype(jnp.bfloat16)
+
+    def within(first, count):
+        return jnp.logical_and(win_v >= first, win_v < first + count)
+
+    own_y = flag((win_v & 1) == y)
+    own_z = flag(within(2 * z, 2))
+    own_half = flag(within(4 * zhalf, 4))
+
+    def pick(own, a, b):
+        return jnp.where((own > 0)[None], a, b)
+
+    gain = in_gain_ref[...]
+    w_r = jnp.concatenate([w_right_ref[...], w_right_gate_ref[...]], axis=1)
+    k_ids = lax.broadcasted_iota(jnp.int32, (tokens, channels), 0)
+    valid_v = jnp.full((tokens, channels), valid_ref[0], jnp.int32)
+    k_live = k_ids < valid_v
+
+    def edge(flat, weights, first, count):
+        proj = jnp.dot(flat, weights, preferred_element_type=jnp.float32)
+        val = jax.nn.sigmoid(proj[:, channels:]) * proj[:, :channels]
+        val = val.reshape(count, tokens, channels)
+        out = []
+        for r in range(count):
+            row_v = jnp.full((tokens, channels), me * local_rows + first + r, jnp.int32)
+            live = jnp.logical_and(k_live, row_v < valid_v)
+            out.append(jnp.where(live, val[r], 0.0).astype(jnp.bfloat16))
+        return out
+
+    for q in range(CHUNKS):
+        rows = pl.ds(q * step, step)
+        x = x_ref[rows].astype(jnp.float32).reshape(step * tokens, channels)
+        normed = layer_norm(x, gain).astype(jnp.bfloat16)
+        normed_ref[rows] = normed.reshape(step, tokens, channels)
+        for r, e in enumerate(edge(normed, w_r, q * step, step)):
+            right_ref[q * step + r] = e
+        copy(Y1, q).start()
+
+    def combine_y(q):
+        rows = pl.ds(q * step, step)
+        copy(Y1, q).wait_recv()
+        here[rows] = pick(own_y, right_ref[rows, mine], from_y[rows])
+
+    w_l = jnp.concatenate([w_left_ref[...], w_left_gate_ref[...]], axis=1)
+
+    def left_chunk(q):
+        flat = normed_ref[pl.ds(q * step, step)].reshape(step * tokens, channels)
+        for r, e in enumerate(edge(flat, w_l, q * step, step)):
+            left_ref[q * step + r] = e.astype(jnp.float32)
+
+    for q in range(CHUNKS):
+        combine_y(q)
+
+        @pl.when(outer)
+        def _():
+            copy(NEAR, q).start()
+
+        left_chunk(q)
+
+    @pl.when(inner)
+    def _():
+        for q in range(CHUNKS):
+            rows = pl.ds(q * step, step)
+            copy(NEAR, q).wait_recv()
+            best[rows] = pick(own_z, here[rows], near[rows])
+            copy(EXCH, q).start()
+
+    gate_in = normed_ref[:, :width, :]
+    for block in range(1, tokens // width):
+        at_block = flag(win_v[:width] == block)
+        gate_in = pick(at_block, normed_ref[:, block * width : (block + 1) * width, :], gate_in)
+    gate_in = gate_in.reshape(local_rows * width, channels)
+    gate_vals = jax.nn.sigmoid(
+        jnp.dot(gate_in, w_gate_ref[...], preferred_element_type=jnp.float32)
+    )
+
+    for q in range(CHUNKS):
+        rows = pl.ds(q * step, step)
+
+        @pl.when(inner)
+        def _():
+            copy(EXCH, q).wait_recv()
+            win_ref[core, rows, mine] = pick(own_half, best[rows], other[rows])
+            copy(FAR, q).start()
+
+        @pl.when(outer)
+        def _():
+            copy(FAR, q).wait_recv()
+
+        copy(Y2, q).start()
+        copy(C1, q).start()
+
+    def contract(side, q):
+        for r in range(step):
+            row = q * step + r
+            right = win_ref[side, row].astype(jnp.float32)
+            prod_ref[:, pl.ds(side * local_rows + row, 1), :] = jnp.sum(
+                left_ref[...] * right[None], axis=1, keepdims=True
+            )
+
+    for q in range(CHUNKS + 1):
+        if q < CHUNKS:
+            copy(Y2, q).wait_recv()
+            copy(C2, q).start()
+            contract(core, q)
+        if q > 0:
+            copy(C1, q - 1).wait_recv()
+            copy(C2, q - 1).wait_recv()
+            contract(1 - core, q - 1)
+
+    product = prod_ref[...].reshape(local_rows * width, channels)
+    normed_out = layer_norm(product, out_gain_ref[...]).astype(jnp.bfloat16)
+    result = jnp.dot(normed_out, w_out_ref[...], preferred_element_type=jnp.float32)
+    o_ref[...] = (gate_vals * result).astype(jnp.bfloat16).reshape(local_rows, width, channels)
+
+    for q in range(CHUNKS):
+        for kind in (Y1, Y2, C1, C2):
+            copy(kind, q).wait_send()
+
+        @pl.when(outer)
+        def _():
+            copy(NEAR, q).wait_send()
+
+        @pl.when(inner)
+        def _():
+            copy(EXCH, q).wait_send()
+            copy(FAR, q).wait_send()
+
+
+def fused(
+    pair_rows, in_gain, w_left, w_left_gate, w_right, w_right_gate, w_gate, w_out, out_gain, valid_len, window
+):
+    local_rows, tokens, channels = pair_rows.shape
+    width = tokens // 8
+    vmem = pl.BlockSpec(memory_space=pltpu.VMEM)
+    smem = pl.BlockSpec(memory_space=pltpu.SMEM)
+    part = pltpu.VMEM((local_rows, tokens // 2, channels), jnp.bfloat16)
+    return pl.pallas_call(
+        fused_kernel,
+        out_shape=jax.ShapeDtypeStruct((local_rows, width, channels), jnp.bfloat16),
+        in_specs=[smem, smem] + [vmem] * 9,
+        out_specs=vmem,
+        scratch_shapes=[
+            pltpu.VMEM((local_rows, tokens, channels), jnp.bfloat16),
+            pltpu.VMEM((local_rows, tokens, channels), jnp.float32),
+            pltpu.VMEM((local_rows, tokens, channels), jnp.bfloat16),
+            part,
+            part,
+            part,
+            part,
+            part,
+            pltpu.VMEM((2, local_rows, tokens, channels), jnp.bfloat16),
+            pltpu.VMEM((local_rows, width, channels), jnp.float32),
+            pltpu.SemaphoreType.DMA((7, CHUNKS)),
+            pltpu.SemaphoreType.DMA((7, CHUNKS)),
+        ],
+        compiler_params=pltpu.CompilerParams(collective_id=0, has_side_effects=True),
+    )(
+        valid_len,
+        window,
+        pair_rows,
+        in_gain.reshape(1, channels),
+        w_left,
+        w_left_gate,
+        w_right,
+        w_right_gate,
+        w_gate,
+        w_out,
+        out_gain.reshape(1, channels),
+    )
+
+
+def on_device_any(row_devices, pair_rows, *rest):
+    local_rows, tokens, channels = pair_rows.shape
+    fits = row_devices == LINE * 4 and tokens // 8 == 2 * local_rows and local_rows % CHUNKS == 0
+    return (fused if fits else on_device)(pair_rows, *rest)
+
+
 def solution(mesh):
     return jax.shard_map(
-        on_device,
+        functools.partial(on_device_any, mesh.shape["row"]),
         mesh=mesh,
         in_specs=(
             P(("groups", "row"), None, None),

time: 76 us -> 27.8 us (0.37)
  blocking collectives: 48.2 us -> 0 us
  Pallas kernels: 0 us -> 24.9 us
  waiting for transfers between devices: 8.97 us -> 0 us
  starting transfers between devices: 7.41 us -> 0 us
  other arithmetic: 4.38 us -> 0 us
  matrix products: 3.4 us -> 0 us
    all_gather x1 -> x0, blocking collectives: 48.2 us -> none  [on_device(): window_right = lax.all_gather(picked, 'row', axis=1, tiled=True)]
    pallas_call x0 -> x1, Pallas kernels: none -> 24.9 us  [fused(): pl.pallas_call(fused_kernel, out_shape=jax.ShapeDtypeStruct((local_rows,...]
    all_to_all x1 -> x0, waiting for transfers between devices: 8.97 us -> none  [on_device(): lax.all_to_all(right_edge, 'row', split_axis=1, concat_axis=0, tiled=True)]
    all_to_all x1 -> x0, starting transfers between devices: 7.41 us -> none  [on_device(): lax.all_to_all(right_edge, 'row', split_axis=1, concat_axis=0, tiled=True)]
    dot_general x4 -> x0, matrix products: 3.4 us -> none  [the longest x1 1.22 us: on_device(): projected = jnp.dot(flat_rows, joined, preferred_element_type=jnp.float32)]
    reduce_sum x4 -> x0, other arithmetic: 2.69 us -> none  [the longest x2 1.48 us: layer_norm(): variance_v = jnp.mean(centered * centered, axis=-1, keepdims=True)]
    convert_element_type x4 -> x0, other arithmetic: 1.6 us -> none  [the longest x1 1.29 us: on_device(): layer_norm(pair_rows.astype(jnp.float32), in_gain).astype(jnp.bfloat16)]
    unnamed x7 -> x1, local copies, waits for them, and re-layouts: 0.21 us -> 1.38 us
  transfers between devices with their start and end apart: 1 -> 0, of which waited for: 1 -> 0; matrix products, arithmetic and copies ran while one was open for 0% -> 0% of each run, Pallas kernels for 0% -> 0%
where the time goes in v1:
time: 27.8 us; the launch traced here: 27.6 us
  Pallas kernels  24.9 us (90%)
  local copies, waits for them, and re-layouts  1.38 us (5%)
  between operations  1.3 us (5%)
    pallas_call x1, Pallas kernels, fused(): pl.pallas_call(fused_kernel, out_shape=jax.ShapeDtypeStruct((local_rows,...  24.9 us
    unnamed x1, local copies, waits for them, and re-layouts  1.38 us

profile of v1, /device:TPU:0, one launch (start us, length us, event | category | flops | bytes accessed | tf_op | source)
XLA Modules:
  0.0 27.6 jit_solution(8855642434612689824)
XLA Ops:
  1.3 24.9 %shard_map.109 = bf16[8,16,128]{2,1,0:T(8,128)(2,1)} custom-call(s32[1]{0:T(128)S(6)} %copy.13.valid_ref, s32[1]{0:T(128)S(6)} %copy.14.window_ref, bf16[8,128,128]{2,1,0:T(8,128)(2,1)} %x_ref.1, f32[1,128]{1,0:T(1,128)} %bitcast.2, bf16[128,128]{1,0:T(8,128)(2,1)} %w_left_ref.1, bf16[128,128]{1,0:T(8,128)(2,1)} %w_left_gate_ref.1, ...), custom_call_target="tpu_custom_call" | custom-call | tf_op jit(solution)/shard_map/pallas_call | solution.py:303
  26.2 1.4 %copy.15 = bf16[8,16,128]{2,1,0:T(8,128)(2,1)} copy(bf16[8,16,128]{2,1,0:T(8,128)(2,1)} %shard_map.109) | data formatting | bytes 65536

commit v2 on v1

--- a/solution.py
+++ b/solution.py
@@ -70,9 +70,9 @@
 
 
 MESH = pl.DeviceIdType.MESH
-CHUNKS = 4
-LINE = 4
-Y1, NEAR, EXCH, FAR, Y2, C1, C2 = range(7)
+CHUNKS = 2
+QUAD = 4
+QUARTER, CROSS, GATHER, SWAP = 0, 3, 4, 7
 
 
 def fused_kernel(
@@ -91,52 +91,52 @@
     normed_ref,
     left_ref,
     right_ref,
-    from_y,
-    here,
-    near,
+    parts,
     best,
-    other,
+    cross,
     win_ref,
     prod_ref,
     send_sem,
     recv_sem,
 ):
     local_rows, tokens, channels = x_ref.shape
-    half = tokens // 2
+    depth = tokens // QUAD
     width = o_ref.shape[1]
     step = local_rows // CHUNKS
 
     me = lax.axis_index("row")
     core = lax.rem(me, 2)
     chip = lax.div(me, 2)
-    y = lax.rem(chip, 2)
-    z = lax.div(chip, 2)
-    zrem = lax.rem(z, 2)
-    zhalf = lax.div(z, 2)
-
-    def at(z_, y_, core_):
-        return {"row": (z_ * 2 + y_) * 2 + core_}
-
-    y_peer = at(z, 1 - y, core)
-    core_peer = at(z, y, 1 - core)
-    pair_peer = at(zhalf * 2 + 1 - zrem, y, core)
-    inner_peer = at(LINE - 1 - z, y, core)
-    outer = jnp.logical_or(z == 0, z == LINE - 1)
-    inner = jnp.logical_not(outer)
-    mine = pl.ds(pl.multiple_of(y * half, half), half)
-    theirs = pl.ds(pl.multiple_of((1 - y) * half, half), half)
+    quad = lax.div(chip, QUAD)
+    spot = lax.rem(chip, QUAD)
+    y = lax.rem(spot, 2)
+    z = lax.div(spot, 2)
+    spots = ((1 - z) * 2 + 1 - y, (1 - z) * 2 + y, z * 2 + 1 - y)
+
+    def at(quad_, spot_, core_):
+        return {"row": (quad_ * QUAD + spot_) * 2 + core_}
+
+    peers = [at(quad, s, core) for s in spots]
+    cross_peer = at(1 - quad, spot, core)
+    core_peer = at(quad, spot, 1 - core)
+
+    def quarter(s):
+        return pl.ds(pl.multiple_of(s * depth, depth), depth)
+
+    mine = quarter(spot)
 
     def copy(kind, q):
         rows = pl.ds(q * step, step)
-        src, dst, dev = {
-            Y1: (right_ref.at[rows, theirs], from_y.at[rows], y_peer),
-            NEAR: (here.at[rows], near.at[rows], pair_peer),
-            EXCH: (best.at[rows], other.at[rows], inner_peer),
-            FAR: (win_ref.at[core, rows, mine], win_ref.at[core, rows, mine], pair_peer),
-            Y2: (win_ref.at[core, rows, mine], win_ref.at[core, rows, mine], y_peer),
-            C1: (win_ref.at[core, rows, mine], win_ref.at[core, rows, mine], core_peer),
-            C2: (win_ref.at[core, rows, theirs], win_ref.at[core, rows, theirs], core_peer),
-        }[kind]
+        if kind < CROSS:
+            src, dst, dev = right_ref.at[rows, quarter(spots[kind])], parts.at[kind, rows], peers[kind]
+        elif kind == CROSS:
+            src, dst, dev = best.at[rows], cross.at[rows], cross_peer
+        elif kind < SWAP:
+            src = dst = win_ref.at[core, rows, mine]
+            dev = peers[kind - GATHER]
+        else:
+            src = dst = win_ref.at[core, rows]
+            dev = core_peer
         return pltpu.make_async_remote_copy(
             src_ref=src,
             dst_ref=dst,
@@ -147,30 +147,19 @@
         )
 
     barrier = pltpu.get_barrier_semaphore()
-    for peer in (y_peer, core_peer, pair_peer):
+    everyone = peers + [cross_peer, core_peer]
+    for peer in everyone:
         pl.semaphore_signal(barrier, inc=1, device_id=peer, device_id_type=MESH)
-
-    @pl.when(inner)
-    def _():
-        pl.semaphore_signal(barrier, inc=1, device_id=inner_peer, device_id_type=MESH)
-        pl.semaphore_wait(barrier, 4)
-
-    @pl.when(outer)
-    def _():
-        pl.semaphore_wait(barrier, 3)
+    pl.semaphore_wait(barrier, len(everyone))
 
     win = window_ref[0]
-    win_v = jnp.full((half, channels), win, jnp.int32)
+    win_v = jnp.full((depth, channels), win, jnp.int32)
 
     def flag(cond):
         return jnp.where(cond, 1.0, 0.0).astype(jnp.bfloat16)
 
-    def within(first, count):
-        return jnp.logical_and(win_v >= first, win_v < first + count)
-
-    own_y = flag((win_v & 1) == y)
-    own_z = flag(within(2 * z, 2))
-    own_half = flag(within(4 * zhalf, 4))
+    owners = [flag(win_v == quad * QUAD + s) for s in spots]
+    own_quad = flag(jnp.logical_and(win_v >= quad * QUAD, win_v < (quad + 1) * QUAD))
 
     def pick(own, a, b):
         return jnp.where((own > 0)[None], a, b)
@@ -199,12 +188,8 @@
         normed_ref[rows] = normed.reshape(step, tokens, channels)
         for r, e in enumerate(edge(normed, w_r, q * step, step)):
             right_ref[q * step + r] = e
-        copy(Y1, q).start()
-
-    def combine_y(q):
-        rows = pl.ds(q * step, step)
-        copy(Y1, q).wait_recv()
-        here[rows] = pick(own_y, right_ref[rows, mine], from_y[rows])
+        for t in range(3):
+            copy(QUARTER + t, q).start()
 
     w_l = jnp.concatenate([w_left_ref[...], w_left_gate_ref[...]], axis=1)
 
@@ -214,21 +199,14 @@
             left_ref[q * step + r] = e.astype(jnp.float32)
 
     for q in range(CHUNKS):
-        combine_y(q)
-
-        @pl.when(outer)
-        def _():
-            copy(NEAR, q).start()
-
+        rows = pl.ds(q * step, step)
+        held = right_ref[rows, mine]
+        for t in range(3):
+            copy(QUARTER + t, q).wait_recv()
+            held = pick(owners[t], parts[t, rows], held)
+        best[rows] = held
+        copy(CROSS, q).start()
         left_chunk(q)
-
-    @pl.when(inner)
-    def _():
-        for q in range(CHUNKS):
-            rows = pl.ds(q * step, step)
-            copy(NEAR, q).wait_recv()
-            best[rows] = pick(own_z, here[rows], near[rows])
-            copy(EXCH, q).start()
 
     gate_in = normed_ref[:, :width, :]
     for block in range(1, tokens // width):
@@ -241,19 +219,10 @@
 
     for q in range(CHUNKS):
         rows = pl.ds(q * step, step)
-
-        @pl.when(inner)
-        def _():
-            copy(EXCH, q).wait_recv()
-            win_ref[core, rows, mine] = pick(own_half, best[rows], other[rows])
-            copy(FAR, q).start()
-
-        @pl.when(outer)
-        def _():
-            copy(FAR, q).wait_recv()
-
-        copy(Y2, q).start()
-        copy(C1, q).start()
+        copy(CROSS, q).wait_recv()
+        win_ref[core, rows, mine] = pick(own_quad, best[rows], cross[rows])
+        for t in range(3):
+            copy(GATHER + t, q).start()
 
     def contract(side, q):
         for r in range(step):
@@ -265,12 +234,12 @@
 
     for q in range(CHUNKS + 1):
         if q < CHUNKS:
-            copy(Y2, q).wait_recv()
-            copy(C2, q).start()
+            for t in range(3):
+                copy(GATHER + t, q).wait_recv()
+            copy(SWAP, q).start()
             contract(core, q)
         if q > 0:
-            copy(C1, q - 1).wait_recv()
-            copy(C2, q - 1).wait_recv()
+            copy(SWAP, q - 1).wait_recv()
             contract(1 - core, q - 1)
 
     product = prod_ref[...].reshape(local_rows * width, channels)
@@ -279,17 +248,8 @@
     o_ref[...] = (gate_vals * result).astype(jnp.bfloat16).reshape(local_rows, width, channels)
 
     for q in range(CHUNKS):
-        for kind in (Y1, Y2, C1, C2):
+        for kind in range(SWAP + 1):
             copy(kind, q).wait_send()
-
-        @pl.when(outer)
-        def _():
-            copy(NEAR, q).wait_send()
-
-        @pl.when(inner)
-        def _():
-            copy(EXCH, q).wait_send()
-            copy(FAR, q).wait_send()
 
 
 def fused(
@@ -299,7 +259,7 @@
     width = tokens // 8
     vmem = pl.BlockSpec(memory_space=pltpu.VMEM)
     smem = pl.BlockSpec(memory_space=pltpu.SMEM)
-    part = pltpu.VMEM((local_rows, tokens // 2, channels), jnp.bfloat16)
+    part = (local_rows, tokens // QUAD, channels)
     return pl.pallas_call(
         fused_kernel,
         out_shape=jax.ShapeDtypeStruct((local_rows, width, channels), jnp.bfloat16),
@@ -309,15 +269,13 @@
             pltpu.VMEM((local_rows, tokens, channels), jnp.bfloat16),
             pltpu.VMEM((local_rows, tokens, channels), jnp.float32),
             pltpu.VMEM((local_rows, tokens, channels), jnp.bfloat16),
-            part,
-            part,
-            part,
-            part,
-            part,
+            pltpu.VMEM((3, *part), jnp.bfloat16),
+            pltpu.VMEM(part, jnp.bfloat16),
+            pltpu.VMEM(part, jnp.bfloat16),
             pltpu.VMEM((2, local_rows, tokens, channels), jnp.bfloat16),
             pltpu.VMEM((local_rows, width, channels), jnp.float32),
-            pltpu.SemaphoreType.DMA((7, CHUNKS)),
-            pltpu.SemaphoreType.DMA((7, CHUNKS)),
+            pltpu.SemaphoreType.DMA((SWAP + 1, CHUNKS)),
+            pltpu.SemaphoreType.DMA((SWAP + 1, CHUNKS)),
         ],
         compiler_params=pltpu.CompilerParams(collective_id=0, has_side_effects=True),
     )(
@@ -337,7 +295,7 @@
 
 def on_device_any(row_devices, pair_rows, *rest):
     local_rows, tokens, channels = pair_rows.shape
-    fits = row_devices == LINE * 4 and tokens // 8 == 2 * local_rows and local_rows % CHUNKS == 0
+    fits = row_devices == QUAD * 4 and tokens // 8 == 2 * local_rows and local_rows % CHUNKS == 0
     return (fused if fits else on_device)(pair_rows, *rest)
 
 

time: 27.8 us -> 23.3 us (0.84)
  the two profiles are of different devices: /device:TPU:0 before, /device:TPU:1 now
where the time goes in v2:
time: 23.3 us; the launch traced here: 23.1 us
  Pallas kernels  20.4 us (88%)
  local copies, waits for them, and re-layouts  1.38 us (6%)
  between operations  1.3 us (6%)
    pallas_call x1, Pallas kernels, fused(): pl.pallas_call(fused_kernel, out_shape=jax.ShapeDtypeStruct((local_rows,...  20.4 us
    unnamed x1, local copies, waits for them, and re-layouts  1.38 us

profile of v2, /device:TPU:1, one launch (start us, length us, event | category | flops | bytes accessed | tf_op | source)
XLA Modules:
  0.0 23.1 jit_solution(9758944410152905404)
XLA Ops:
  1.3 20.4 %shard_map.109 = bf16[8,16,128]{2,1,0:T(8,128)(2,1)} custom-call(s32[1]{0:T(128)S(6)} %copy.13.valid_ref, s32[1]{0:T(128)S(6)} %copy.14.window_ref, bf16[8,128,128]{2,1,0:T(8,128)(2,1)} %x_ref.1, f32[1,128]{1,0:T(1,128)} %bitcast.2, bf16[128,128]{1,0:T(8,128)(2,1)} %w_left_ref.1, bf16[128,128]{1,0:T(8,128)(2,1)} %w_left_gate_ref.1, ...), custom_call_target="tpu_custom_call" | custom-call | tf_op jit(solution)/shard_map/pallas_call | solution.py:263
  21.7 1.4 %copy.15 = bf16[8,16,128]{2,1,0:T(8,128)(2,1)} copy(bf16[8,16,128]{2,1,0:T(8,128)(2,1)} %shard_map.109) | data formatting | bytes 65536

commit v3 on v2

--- a/solution.py
+++ b/solution.py
@@ -78,6 +78,16 @@
 def fused_kernel(
     valid_ref,
     window_ref,
+    x_hbm,
+    in_gain_hbm,
+    w_left_hbm,
+    w_left_gate_hbm,
+    w_right_hbm,
+    w_right_gate_hbm,
+    w_gate_hbm,
+    w_out_hbm,
+    out_gain_hbm,
+    o_ref,
     x_ref,
     in_gain_ref,
     w_left_ref,
@@ -87,10 +97,8 @@
     w_gate_ref,
     w_out_ref,
     out_gain_ref,
-    o_ref,
     normed_ref,
     left_ref,
-    right_ref,
     parts,
     best,
     cross,
@@ -98,6 +106,7 @@
     prod_ref,
     send_sem,
     recv_sem,
+    load_sem,
 ):
     local_rows, tokens, channels = x_ref.shape
     depth = tokens // QUAD
@@ -128,7 +137,7 @@
     def copy(kind, q):
         rows = pl.ds(q * step, step)
         if kind < CROSS:
-            src, dst, dev = right_ref.at[rows, quarter(spots[kind])], parts.at[kind, rows], peers[kind]
+            src, dst, dev = x_hbm.at[rows, quarter(spots[kind])], parts.at[kind, rows], peers[kind]
         elif kind == CROSS:
             src, dst, dev = best.at[rows], cross.at[rows], cross_peer
         elif kind < SWAP:
@@ -150,7 +159,30 @@
     everyone = peers + [cross_peer, core_peer]
     for peer in everyone:
         pl.semaphore_signal(barrier, inc=1, device_id=peer, device_id_type=MESH)
+    loads = [
+        pltpu.make_async_copy(src, dst, load_sem.at[n])
+        for n, (src, dst) in enumerate(
+            (
+                (x_hbm, x_ref),
+                (in_gain_hbm, in_gain_ref),
+                (w_left_hbm, w_left_ref),
+                (w_left_gate_hbm, w_left_gate_ref),
+                (w_gate_hbm, w_gate_ref),
+                (w_right_hbm, w_right_ref),
+                (w_right_gate_hbm, w_right_gate_ref),
+                (w_out_hbm, w_out_ref),
+                (out_gain_hbm, out_gain_ref),
+            )
+        )
+    ]
+    for load in loads:
+        load.start()
     pl.semaphore_wait(barrier, len(everyone))
+    for q in range(CHUNKS):
+        for t in range(3):
+            copy(QUARTER + t, q).start()
+    for load in loads:
+        load.wait()
 
     win = window_ref[0]
     win_v = jnp.full((depth, channels), win, jnp.int32)
@@ -170,42 +202,32 @@
     valid_v = jnp.full((tokens, channels), valid_ref[0], jnp.int32)
     k_live = k_ids < valid_v
 
-    def edge(flat, weights, first, count):
+    def normal(rows):
+        flat = rows.astype(jnp.float32).reshape(step * tokens, channels)
+        return layer_norm(flat, gain).astype(jnp.bfloat16)
+
+    def edge(flat, weights, row_v):
         proj = jnp.dot(flat, weights, preferred_element_type=jnp.float32)
         val = jax.nn.sigmoid(proj[:, channels:]) * proj[:, :channels]
-        val = val.reshape(count, tokens, channels)
+        val = val.reshape(step, tokens, channels)
         out = []
-        for r in range(count):
-            row_v = jnp.full((tokens, channels), me * local_rows + first + r, jnp.int32)
-            live = jnp.logical_and(k_live, row_v < valid_v)
-            out.append(jnp.where(live, val[r], 0.0).astype(jnp.bfloat16))
+        for r in range(step):
+            live = jnp.logical_and(k_live, row_v + r < valid_v)
+            rounded = jnp.where(live, val[r], 0.0).astype(jnp.bfloat16)
+            out.append(rounded.astype(jnp.float32))
         return out
 
-    for q in range(CHUNKS):
+    w_l = jnp.concatenate([w_left_ref[...], w_left_gate_ref[...]], axis=1)
+
+    def left_chunk(q):
         rows = pl.ds(q * step, step)
-        x = x_ref[rows].astype(jnp.float32).reshape(step * tokens, channels)
-        normed = layer_norm(x, gain).astype(jnp.bfloat16)
-        normed_ref[rows] = normed.reshape(step, tokens, channels)
-        for r, e in enumerate(edge(normed, w_r, q * step, step)):
-            right_ref[q * step + r] = e
-        for t in range(3):
-            copy(QUARTER + t, q).start()
-
-    w_l = jnp.concatenate([w_left_ref[...], w_left_gate_ref[...]], axis=1)
-
-    def left_chunk(q):
-        flat = normed_ref[pl.ds(q * step, step)].reshape(step * tokens, channels)
-        for r, e in enumerate(edge(flat, w_l, q * step, step)):
-            left_ref[q * step + r] = e.astype(jnp.float32)
-
-    for q in range(CHUNKS):
-        rows = pl.ds(q * step, step)
-        held = right_ref[rows, mine]
-        for t in range(3):
-            copy(QUARTER + t, q).wait_recv()
-            held = pick(owners[t], parts[t, rows], held)
-        best[rows] = held
-        copy(CROSS, q).start()
+        flat = normal(x_ref[rows])
+        normed_ref[rows] = flat.reshape(step, tokens, channels)
+        row_v = jnp.full((tokens, channels), me * local_rows + q * step, jnp.int32)
+        for r, e in enumerate(edge(flat, w_l, row_v)):
+            left_ref[q * step + r] = e
+
+    for q in range(CHUNKS):
         left_chunk(q)
 
     gate_in = normed_ref[:, :width, :]
@@ -219,16 +241,26 @@
 
     for q in range(CHUNKS):
         rows = pl.ds(q * step, step)
+        held = x_ref[rows, mine]
+        for t in range(3):
+            copy(QUARTER + t, q).wait_recv()
+            held = pick(owners[t], parts[t, rows], held)
+        best[rows] = held
+        copy(CROSS, q).start()
+
+    for q in range(CHUNKS):
+        rows = pl.ds(q * step, step)
         copy(CROSS, q).wait_recv()
         win_ref[core, rows, mine] = pick(own_quad, best[rows], cross[rows])
         for t in range(3):
             copy(GATHER + t, q).start()
 
     def contract(side, q):
-        for r in range(step):
-            row = q * step + r
-            right = win_ref[side, row].astype(jnp.float32)
-            prod_ref[:, pl.ds(side * local_rows + row, 1), :] = jnp.sum(
+        first = side * local_rows + q * step
+        row_v = jnp.full((tokens, channels), win * width + first, jnp.int32)
+        flat = normal(win_ref[side, pl.ds(q * step, step)])
+        for r, right in enumerate(edge(flat, w_r, row_v)):
+            prod_ref[:, pl.ds(first + r, 1), :] = jnp.sum(
                 left_ref[...] * right[None], axis=1, keepdims=True
             )
 
@@ -263,12 +295,15 @@
     return pl.pallas_call(
         fused_kernel,
         out_shape=jax.ShapeDtypeStruct((local_rows, width, channels), jnp.bfloat16),
-        in_specs=[smem, smem] + [vmem] * 9,
+        in_specs=[smem, smem] + [pl.BlockSpec(memory_space=pl.ANY)] * 9,
         out_specs=vmem,
         scratch_shapes=[
             pltpu.VMEM((local_rows, tokens, channels), jnp.bfloat16),
+            pltpu.VMEM((1, channels), jnp.float32),
+            *[pltpu.VMEM((channels, channels), jnp.bfloat16)] * 6,
+            pltpu.VMEM((1, channels), jnp.float32),
+            pltpu.VMEM((local_rows, tokens, channels), jnp.bfloat16),
             pltpu.VMEM((local_rows, tokens, channels), jnp.float32),
-            pltpu.VMEM((local_rows, tokens, channels), jnp.bfloat16),
             pltpu.VMEM((3, *part), jnp.bfloat16),
             pltpu.VMEM(part, jnp.bfloat16),
             pltpu.VMEM(part, jnp.bfloat16),
@@ -276,6 +311,7 @@
             pltpu.VMEM((local_rows, width, channels), jnp.float32),
             pltpu.SemaphoreType.DMA((SWAP + 1, CHUNKS)),
             pltpu.SemaphoreType.DMA((SWAP + 1, CHUNKS)),
+            pltpu.SemaphoreType.DMA((9,)),
         ],
         compiler_params=pltpu.CompilerParams(collective_id=0, has_side_effects=True),
     )(

time: 23.3 us -> 22.8 us (0.979)
  the two profiles are of different devices: /device:TPU:1 before, /device:TPU:0 now
where the time goes in v3:
time: 22.8 us; the launch traced here: 22.6 us
  Pallas kernels  19.9 us (87%)
  local copies, waits for them, and re-layouts  1.38 us (6%)
  between operations  1.3 us (6%)
    pallas_call x1, Pallas kernels, fused(): pl.pallas_call(fused_kernel, out_shape=jax.ShapeDtypeStruct((local_rows,...  19.9 us
    unnamed x1, local copies, waits for them, and re-layouts  1.38 us

profile of v3, /device:TPU:0, one launch (start us, length us, event | category | flops | bytes accessed | tf_op | source)
XLA Modules:
  0.0 22.6 jit_solution(8630655524481868001)
XLA Ops:
  1.3 19.9 %shard_map.109 = bf16[8,16,128]{2,1,0:T(8,128)(2,1)} custom-call(s32[1]{0:T(128)S(6)} %copy.13.valid_ref, s32[1]{0:T(128)S(6)} %copy.14.window_ref, bf16[8,128,128]{2,1,0:T(8,128)(2,1)} %x_hbm.1, f32[1,128]{1,0:T(1,128)} %bitcast.2, bf16[128,128]{1,0:T(8,128)(2,1)} %w_left_hbm.1, bf16[128,128]{1,0:T(8,128)(2,1)} %w_left_gate_hbm.1, ...), custom_call_target="tpu_custom_call" | custom-call | tf_op jit(solution)/shard_map/pallas_call | solution.py:295
  21.2 1.4 %copy.15 = bf16[8,16,128]{2,1,0:T(8,128)(2,1)} copy(bf16[8,16,128]{2,1,0:T(8,128)(2,1)} %shard_map.109) | data formatting | bytes 65536

commit v4 on v3

--- a/solution.py
+++ b/solution.py
@@ -137,7 +137,7 @@
     def copy(kind, q):
         rows = pl.ds(q * step, step)
         if kind < CROSS:
-            src, dst, dev = x_hbm.at[rows, quarter(spots[kind])], parts.at[kind, rows], peers[kind]
+            src, dst, dev = x_ref.at[rows, quarter(spots[kind])], parts.at[kind, rows], peers[kind]
         elif kind == CROSS:
             src, dst, dev = best.at[rows], cross.at[rows], cross_peer
         elif kind < SWAP:
@@ -163,7 +163,7 @@
         pltpu.make_async_copy(src, dst, load_sem.at[n])
         for n, (src, dst) in enumerate(
             (
-                (x_hbm, x_ref),
+                *((x_hbm.at[pl.ds(q * step, step)], x_ref.at[pl.ds(q * step, step)]) for q in range(CHUNKS)),
                 (in_gain_hbm, in_gain_ref),
                 (w_left_hbm, w_left_ref),
                 (w_left_gate_hbm, w_left_gate_ref),
@@ -179,9 +179,10 @@
         load.start()
     pl.semaphore_wait(barrier, len(everyone))
     for q in range(CHUNKS):
+        loads[q].wait()
         for t in range(3):
             copy(QUARTER + t, q).start()
-    for load in loads:
+    for load in loads[CHUNKS:]:
         load.wait()
 
     win = window_ref[0]
@@ -311,7 +312,7 @@
             pltpu.VMEM((local_rows, width, channels), jnp.float32),
             pltpu.SemaphoreType.DMA((SWAP + 1, CHUNKS)),
             pltpu.SemaphoreType.DMA((SWAP + 1, CHUNKS)),
-            pltpu.SemaphoreType.DMA((9,)),
+            pltpu.SemaphoreType.DMA((8 + CHUNKS,)),
         ],
         compiler_params=pltpu.CompilerParams(collective_id=0, has_side_effects=True),
     )(

time: 22.8 us -> 22.6 us (level)
  no operation moved by 1% of the time
where the time goes in v4:
time: 22.6 us; the launch traced here: 22.4 us
  Pallas kernels  19.7 us (87%)
  local copies, waits for them, and re-layouts  1.38 us (6%)
  between operations  1.3 us (6%)
    pallas_call x1, Pallas kernels, fused(): pl.pallas_call(fused_kernel, out_shape=jax.ShapeDtypeStruct((local_rows,...  19.7 us
    unnamed x1, local copies, waits for them, and re-layouts  1.38 us

profile of v4, /device:TPU:0, one launch (start us, length us, event | category | flops | bytes accessed | tf_op | source)
XLA Modules:
  0.0 22.4 jit_solution(15678620986074373126)
XLA Ops:
  1.3 19.7 %shard_map.109 = bf16[8,16,128]{2,1,0:T(8,128)(2,1)} custom-call(s32[1]{0:T(128)S(6)} %copy.13.valid_ref, s32[1]{0:T(128)S(6)} %copy.14.window_ref, bf16[8,128,128]{2,1,0:T(8,128)(2,1)} %x_hbm.1, f32[1,128]{1,0:T(1,128)} %bitcast.2, bf16[128,128]{1,0:T(8,128)(2,1)} %w_left_hbm.1, bf16[128,128]{1,0:T(8,128)(2,1)} %w_left_gate_hbm.1, ...), custom_call_target="tpu_custom_call" | custom-call | tf_op jit(solution)/shard_map/pallas_call | solution.py:296
  21.0 1.4 %copy.15 = bf16[8,16,128]{2,1,0:T(8,128)(2,1)} copy(bf16[8,16,128]{2,1,0:T(8,128)(2,1)} %shard_map.109) | data formatting | bytes 65536
